TPU v7x, 256 devices: a whole 4x4x8 slice. The times are simulated.
256 devices in a mesh: tok: 64 (over y, z, core), head: 4 (over x).
Axes of the slice: x: 4, y: 4, z: 8, core: 2. Of those that a mesh axis runs over, the one named last changes fastest.
Arguments:
- query_rows: bfloat16 [32768, 4, 1024], P('tok', 'head'), may hold values from -6 to 6
- key_rows: bfloat16 [32768, 4, 128], P('tok', 'head'), may hold values from -6 to 6
- value_rows: bfloat16 [32768, 4, 128], P('tok', 'head'), may hold values from -6 to 6
- output_gradient: bfloat16 [32768, 4, 1024], P('tok', 'head'), may hold values from -6 to 6
- row_logsumexp: bfloat16 [4, 8, 32768], P('head', None, 'tok'), may hold values from 3 to 7
- row_delta_sums: bfloat16 [4, 8, 32768], P('head', None, 'tok'), may hold values from -5 to 5
- segments: int32 [32768], replicated, may hold values from 0 to 32767, as said below
- query_key_value_weight: bfloat16 [4096, 4, 1280], P('tok', 'head'), may hold values from -0.09375 to 0.09375
Outputs:
- grad_input: bfloat16 [32768, 4096], P('tok', 'head')
Inputs may be any that keep to these rules, and one draw needn't show every extreme that they name: `segments`: numbers never fall along the tokens, and every document lies inside one window of 512 consecutive tokens.
All inputs are finite; a program needn't handle non-finite values.
Results may differ from a plain program's by a relative error of at most 0.012.
Values may be sent and summed in bfloat16 or wider, within the bound.
No kernel may reach another device: no remote copies, remote signals or barrier semaphores. Data moves between devices by JAX's collectives and lax.ppermute only.
A program may use at most 128 MiB of HBM per device.

v0:
```python
import jax
import jax.numpy as jnp
import numpy as np
from jax import lax
from jax.sharding import PartitionSpec as P

BLOCK = 128


def pair_lists(block_count):
    query_list = []
    key_list = []
    for query_block in range(block_count):
        for key_block in range(query_block + 1):
            query_list.append(query_block)
            key_list.append(key_block)
    return (np.array(query_list, np.int32), np.array(key_list, np.int32))


def live_pairs(seg_window, query_list, key_list, tile_rows):
    first_seg = jnp.take(seg_window, query_list * tile_rows)
    last_seg = jnp.take(seg_window, key_list * tile_rows + tile_rows - 1)
    return (first_seg == last_seg) | jnp.asarray(query_list == key_list)


def pair_grads(query_tile, dout_tile, key_tile, value_tile, lse_tile, delta_tile, allowed):
    tile_rows, groups, query_width = query_tile.shape
    head_size = key_tile.shape[2]
    heads_per_group = query_width // head_size
    query_heads = query_tile.reshape(tile_rows, groups, heads_per_group, head_size)
    dout_heads = dout_tile.reshape(tile_rows, groups, heads_per_group, head_size)
    scores = jnp.einsum(
        "agrd,bgd->grab", query_heads, key_tile, preferred_element_type=jnp.float32
    ) * head_size ** (-0.5)
    logits = scores - lse_tile.astype(jnp.float32)[:, :, :, None]
    soft_probs = jnp.where(allowed[None, None], jnp.exp(logits), 0.0)
    probs_low = soft_probs.astype(jnp.bfloat16)
    value_gradient = jnp.einsum(
        "grab,agrd->bgd", probs_low, dout_heads, preferred_element_type=jnp.float32
    )
    grad_prob = jnp.einsum(
        "agrd,bgd->grab", dout_heads, value_tile, preferred_element_type=jnp.float32
    )
    grad_score = (soft_probs * (grad_prob - delta_tile.astype(jnp.float32)[:, :, :, None])).astype(
        jnp.bfloat16
    )
    query_gradient = jnp.einsum(
        "grab,bgd->agrd", grad_score, key_tile, preferred_element_type=jnp.float32
    )
    key_gradient = jnp.einsum(
        "grab,agrd->bgd", grad_score, query_heads, preferred_element_type=jnp.float32
    )
    return (query_gradient.reshape(tile_rows, groups, query_width), key_gradient, value_gradient)


def on_device(
    query_rows,
    key_rows,
    value_rows,
    output_gradient,
    row_logsumexp,
    row_delta_sums,
    segments,
    query_key_value_weight,
):
    weight_whole = lax.all_gather(query_key_value_weight, "tok", axis=0, tiled=True)
    window, kv_dev, query_width = query_rows.shape
    head_size = key_rows.shape[2]
    tile_rows = BLOCK
    block_count = window // tile_rows
    query_list, key_list = pair_lists(block_count)
    query_table = jnp.asarray(query_list)
    key_table = jnp.asarray(key_list)
    myself = lax.axis_index("tok")
    own_seg = lax.dynamic_slice_in_dim(segments, myself * window, window)
    own_live = live_pairs(own_seg, query_list, key_list, tile_rows)
    block_ids = jnp.arange(block_count, dtype=jnp.int32)
    query_match = (query_table[:, None] == block_ids[None, :]) & own_live[:, None]
    key_match = key_table[:, None] == block_ids[None, :]
    block_local = jnp.any(query_match[:, :, None] & key_match[:, None, :], axis=0)
    token_local = jnp.repeat(jnp.repeat(block_local, tile_rows, axis=0), tile_rows, axis=1)
    offsets = jnp.arange(window, dtype=jnp.int32)
    allowed_all = (
        (own_seg[:, None] == own_seg[None, :])
        & (offsets[None, :] <= offsets[:, None])
        & token_local
    )
    local_out = pair_grads(
        query_rows,
        output_gradient,
        key_rows,
        value_rows,
        row_logsumexp,
        row_delta_sums,
        allowed_all,
    )
    acc_query = local_out[0].reshape(block_count, tile_rows, kv_dev, query_width)
    acc_key = local_out[1].reshape(block_count, tile_rows, kv_dev, head_size)
    acc_value = local_out[2].reshape(block_count, tile_rows, kv_dev, head_size)
    score_scale = head_size ** (-0.5)
    query_gradient = (acc_query * score_scale).reshape(window, kv_dev, query_width)
    key_gradient = (acc_key * score_scale).reshape(window, kv_dev, head_size)
    value_gradient = acc_value.reshape(window, kv_dev, head_size)
    stacked_gradients = (
        jnp.concatenate([query_gradient, key_gradient, value_gradient], axis=2)
        .astype(jnp.bfloat16)
        .reshape(window, -1)
    )
    flat_piece = weight_whole.reshape(weight_whole.shape[0], -1)
    partial_sum = lax.dot_general(
        stacked_gradients, flat_piece, (((1,), (1,)), ((), ())), preferred_element_type=jnp.float32
    )
    summed = lax.psum_scatter(
        partial_sum.astype(jnp.bfloat16), "head", scatter_dimension=1, tiled=True
    )
    return summed


def solution(mesh):
    placed = (
        P("tok", "head", None),
        P("tok", "head", None),
        P("tok", "head", None),
        P("tok", "head", None),
        P("head", None, "tok"),
        P("head", None, "tok"),
        P(),
        P("tok", "head", None),
    )
    return jax.shard_map(
        on_device, mesh=mesh, in_specs=placed, out_specs=P("tok", "head"), check_vma=False
    )
```

profile of v0, /device:TPU:1, one launch (start us, length us, event | category | flops | bytes accessed | tf_op | source)
XLA Modules:
  0.0 165.1 jit_solution(10995759829409910202)
XLA Ops:
  6.5 0.7 all-gather.2.cloned.1.call-update
  7.3 0.8 dynamic_slice.3
  8.1 0.7 pad_clamp_fusion.1
  8.7 0.7 gather_fusion
  9.4 0.7 pad_clamp_fusion
  10.1 0.7 gather_fusion.1
  10.7 0.7 compare_or_fusion
  11.4 0.7 iota_compare_fusion.1
  12.1 0.2 and_reduce_fusion
  12.2 0.1 copy.22
  12.3 0.1 broadcast_bitcast_fusion
  12.4 0.2 fusion.29
  12.7 1.5 copy.36
  14.2 1.5 copy.37
  15.7 0.7 bitcast_convert_fusion.1
  16.4 0.7 bitcast_convert_fusion
  17.1 1.2 fusion.32
  18.3 2.8 %fusion.11 = bf16[8,512,512]{1,2,0:T(8,128)(2,1)S(1)} fusion(f32[512,512,8]{1,0,2:T(8,128)S(1)} %fusion.32, f32[8,512]{1,0:T(8,128)S(1)} %bitcast_convert_fusion, f32[8,512]{1,0:T(8,128)S(1)} %bitcast_convert_fusion.1, pred[512,512]{0,1:T(8,128)(4,1)S(1)} %fusion.29, bf16[512,8,128]{0,2,1:T(8,128)(2,1)S(1)} %bitcast.99, bf16[512,1,128]{2,0,1:T(8,128)(2,1)S(1)} %copy-done.1), kind=kOutput, calls=%fused_computation.13 | convolution fusion | flops 549453824 | bytes 14057472 | tf_op jit(solution)/shard_map/agrd,bgd->grab/dot_general | solution.py:41
  21.2 0.8 multiply_convert_fusion
  22.0 2.1 %fusion.27 = bf16[512,128]{0,1:T(8,128)(2,1)} fusion(bf16[8,512,512]{1,2,0:T(8,128)(2,1)S(1)} %fusion.11, bf16[512,8,128]{0,2,1:T(8,128)(2,1)S(1)} %bitcast.98), kind=kOutput, calls=%fused_computation.26 | convolution fusion | flops 537001984 | bytes 5373952 | tf_op jit(solution)/shard_map/grab,agrd->bgd/dot_general | solution.py:50
  24.1 1.9 %fusion.24 = bf16[512,128]{0,1:T(8,128)(2,1)S(1)} fusion(bf16[512,8,128]{0,2,1:T(8,128)(2,1)S(1)} %bitcast.100, f32[512,512,8]{1,0,2:T(8,128)S(1)} %fusion.32, f32[8,512]{1,0:T(8,128)S(1)} %bitcast_convert_fusion.1, pred[512,512]{0,1:T(8,128)(4,1)S(1)} %fusion.29), kind=kOutput, calls=%fused_computation.25 | convolution fusion | flops 545325056 | bytes 9846784 | tf_op jit(solution)/shard_map/grab,agrd->bgd/dot_general | solution.py:38
  26.0 74.8 %all-gather.2.cloned.1.call-done = bf16[4096,1,1280]{2,0,1:T(8,128)(2,1)} async-done(((bf16[64,1,1280]{2,0,1:T(8,128)(2,1)}), bf16[4096,1,1280]{2,0,1:T(8,128)(2,1)}) %all-gather.2.cloned.1.call-update) | async-done | bytes 10485776 | tf_op jit(solution)/shard_map/all_gather | solution.py:66
  100.8 11.2 %fusion.7 = bf16[512,4096]{1,0:T(8,128)(2,1)} fusion(bf16[4096,1,1280]{2,0,1:T(8,128)(2,1)} %all-gather.2.cloned.1.call-done, bf16[512,128]{0,1:T(8,128)(2,1)S(1)} %fusion.24, bf16[512,128]{0,1:T(8,128)(2,1)S(1)} %copy-done.2, bf16[512,1024]{0,1:T(8,128)(2,1)S(1)} %bitcast.101), kind=kOutput, calls=%fused_computation.11 | convolution fusion | flops 5374738432 | bytes 15990784 | tf_op jit(solution)/shard_map/dot_general | solution.py:110
  112.1 46.1 %reduce-scatter.2.cloned.1.call-done = bf16[512,1024]{1,0:T(8,128)(2,1)} async-done(((bf16[512,4096]{1,0:T(8,128)(2,1)}), bf16[512,1024]{1,0:T(8,128)(2,1)}) %reduce-scatter.2.cloned.1.call-update) | async-done | bytes 1048592 | tf_op jit(solution)/shard_map/reduce_scatter | solution.py:113
  (10 shorter events, 0.1 us)
Async XLA Ops:
  6.5 10.5 %copy-start = (bf16[512,1,128]{2,0,1:T(8,128)(2,1)S(1)}, bf16[512,1,128]{2,0,1:T(8,128)(2,1)}, u32[]{:S(2)}) copy-start(bf16[512,1,128]{2,0,1:T(8,128)(2,1)} %param.16) | copy-start | bytes 393220
  6.5 11.8 %copy-start.1 = (bf16[512,1,128]{2,0,1:T(8,128)(2,1)S(1)}, bf16[512,1,128]{2,0,1:T(8,128)(2,1)}, u32[]{:S(2)}) copy-start(bf16[512,1,128]{2,0,1:T(8,128)(2,1)} %param.17) | copy-start | bytes 393220
  6.5 94.3 %all-gather.2.cloned.1.call-start = ((), (), s32[]{:S(2)}) async-start(), calls=%async_computation.1 | async-start | bytes 10649600 | tf_op jit(solution)/shard_map/all_gather | solution.py:66
  7.3 151.0 %reduce-scatter.2.cloned.1.call-start = ((), (), s32[]{:S(2)}) async-start(), calls=%async_computation.2 | async-start | bytes 5242880 | tf_op jit(solution)/shard_map/reduce_scatter | solution.py:113
  24.1 76.7 %copy-start.2 = (bf16[512,128]{0,1:T(8,128)(2,1)S(1)}, bf16[512,128]{0,1:T(8,128)(2,1)}, u32[]{:S(2)}) copy-start(bf16[512,128]{0,1:T(8,128)(2,1)} %fusion.27) | copy-start | bytes 393220
Sparse Core Ops, SparseCore 0:
  10.1 90.6 all-gather.1
  112.2 45.9 reduce-scatter.1
where the time goes:
time: 165 us
  waiting for transfers between devices  122 us (74%)
  matrix products  20.1 us (12%)
  between operations  13.5 us (8%)
  local copies, waits for them, and re-layouts  5.3 us (3%)
  other arithmetic  4.45 us (3%)
    all_gather x1, waiting for transfers between devices, on_device(): lax.all_gather(query_key_value_weight, 'tok', axis=0, tiled=True)  74.8 us
    reduce_scatter x1, waiting for transfers between devices, on_device(): lax.psum_scatter(partial_sum.astype(jnp.bfloat16), 'head', scatter_dimens...  46.1 us
    dot_general x1, matrix products, on_device(): lax.dot_general(stacked_gradients, flat_piece, (((1,), (1,)), ((), ())),...  11.2 us
  transfers between devices with their start and end apart: 2, of which 2 were waited for; matrix products, arithmetic and copies ran while one was open for 11% of the time, Pallas kernels for 0%

commit v1 on v0

--- a/solution.py
+++ b/solution.py
@@ -63,7 +63,9 @@
     segments,
     query_key_value_weight,
 ):
-    weight_whole = lax.all_gather(query_key_value_weight, "tok", axis=0, tiled=True)
+    moved = jnp.stack([query_key_value_weight for _ in range(jax.lax.axis_size("tok"))], 0)
+    earlier = jax.lax.all_to_all(moved, "tok", 0, 0)
+    weight_whole = jnp.concatenate(earlier, axis=0)
     window, kv_dev, query_width = query_rows.shape
     head_size = key_rows.shape[2]
     tile_rows = BLOCK

time: 165 us -> 321 us (1.95)
  waiting for transfers between devices: 122 us -> 264 us
  starting transfers between devices: 0.04 us -> 13.5 us
  local copies, waits for them, and re-layouts: 5.3 us -> 9.48 us
  other arithmetic: 4.45 us -> 0.42 us
    all_to_all x0 -> x1, waiting for transfers between devices: none -> 218 us  [on_device(): earlier = jax.lax.all_to_all(moved, 'tok', 0, 0)]
    all_gather x1 -> x0, waiting for transfers between devices: 74.8 us -> none  [on_device(): lax.all_gather(query_key_value_weight, 'tok', axis=0, tiled=True)]
    all_to_all x0 -> x1, starting transfers between devices: none -> 13.5 us  [on_device(): earlier = jax.lax.all_to_all(moved, 'tok', 0, 0)]
    another operation x2 -> x3, local copies, waits for them, and re-layouts: 3 us -> 7.12 us  [the longest x1 6.04 us: on_device(): jnp.stack([query_key_value_weight for _ in range(jax.lax.axis_size('tok')...]
  transfers between devices with their start and end apart: 2 -> 2, of which waited for: 2 -> 2; matrix products, arithmetic and copies ran while one was open for 11% -> 4% of each run, Pallas kernels for 0% -> 0%
where the time goes in v1:
time: 321 us
  waiting for transfers between devices  264 us (82%)
  matrix products  20 us (6%)
  between operations  13.6 us (4%)
  starting transfers between devices  13.5 us (4%)
  local copies, waits for them, and re-layouts  9.48 us (3%)
    all_to_all x1, waiting for transfers between devices, on_device(): earlier = jax.lax.all_to_all(moved, 'tok', 0, 0)  218 us
    reduce_scatter x1, waiting for transfers between devices, on_device(): lax.psum_scatter(partial_sum.astype(jnp.bfloat16), 'head', scatter_dimens...  46.3 us
    all_to_all x1, starting transfers between devices, on_device(): earlier = jax.lax.all_to_all(moved, 'tok', 0, 0)  13.5 us
    dot_general x1, matrix products, on_device(): lax.dot_general(stacked_gradients, flat_piece, (((1,), (1,)), ((), ())),...  11.2 us
  transfers between devices with their start and end apart: 2, of which 2 were waited for; matrix products, arithmetic and copies ran while one was open for 4% of the time, Pallas kernels for 0%

profile of v1, /device:TPU:1, one launch (start us, length us, event | category | flops | bytes accessed | tf_op | source)
XLA Modules:
  0.0 321.2 jit_solution(1353972575943222868)
XLA Ops:
  6.5 6.0 %stack.2 = bf16[64,64,1,1280]{3,1,2,0:T(8,128)(2,1)} broadcast(bf16[64,1280]{1,0:T(8,128)(2,1)} %bitcast.100), dimensions={1,3} | broadcast | bytes 10649600 | tf_op jit(solution)/shard_map/stack | solution.py:66
  12.6 0.0 copy-start.6
  12.6 0.0 copy-start.1
  12.6 0.0 copy-start.4
  12.6 13.5 %all-to-all-start = ((bf16[64,64,1,1280]{3,1,2,0:T(8,128)(2,1)}), bf16[64,64,1,1280]{3,1,2,0:T(8,128)(2,1)}, u32[]{:S(2)}, u32[]{:S(2)}) async-start(bf16[64,64,1,1280]{3,1,2,0:T(8,128)(2,1)} %stack.2), calls=%async_computation | async-start | bytes 20971520 | tf_op jit(solution)/shard_map/all_to_all | solution.py:67
  26.1 0.0 reduce-scatter.2.cloned.1.call-start
  26.2 0.8 dynamic_slice.3
  26.9 0.7 gather_fusion
  27.6 0.7 gather_fusion.1
  28.3 0.2 and_reduce_fusion
  28.5 0.1 copy.30
  28.6 0.1 broadcast_bitcast_fusion
  28.7 0.2 fusion.24
  28.9 0.5 copy.44
  29.5 0.5 copy.45
  30.1 1.2 fusion.27
  31.4 2.8 fusion.6
  34.2 0.8 multiply_convert_fusion
  35.0 2.1 fusion.22
  37.1 1.9 fusion.19
  39.0 217.8 %all-to-all-done = bf16[64,64,1,1280]{3,1,2,0:T(8,128)(2,1)} async-done(((bf16[64,64,1,1280]{3,1,2,0:T(8,128)(2,1)}), bf16[64,64,1,1280]{3,1,2,0:T(8,128)(2,1)}, u32[]{:S(2)}, u32[]{:S(2)}) %all-to-all-start) | async-done | bytes 10485792 | tf_op jit(solution)/shard_map/all_to_all | solution.py:67
  256.9 11.2 %convolution_convert_fusion = bf16[512,4096]{1,0:T(8,128)(2,1)} fusion(bf16[4096,1280]{1,0:T(8,128)(2,1)} %bitcast.21, bf16[512,128]{0,1:T(8,128)(2,1)S(1)} %fusion.19, bf16[512,128]{0,1:T(8,128)(2,1)S(1)} %copy-done.11, bf16[512,1024]{0,1:T(8,128)(2,1)S(1)} %bitcast.99), kind=kOutput, calls=%fused_computation.9 | convolution fusion | flops 5374738432 | bytes 15990784 | tf_op jit(solution)/shard_map/dot_general | solution.py:112
  268.1 0.0 reduce-scatter.2.cloned.1.call-update
  268.1 46.3 %reduce-scatter.2.cloned.1.call-done = bf16[512,1024]{1,0:T(8,128)(2,1)} async-done(((bf16[512,4096]{1,0:T(8,128)(2,1)}), bf16[512,1024]{1,0:T(8,128)(2,1)}) %reduce-scatter.2.cloned.1.call-update) | async-done | bytes 1048592 | tf_op jit(solution)/shard_map/reduce_scatter | solution.py:115
  (28 shorter events, 0.1 us)
Async XLA Ops:
  6.5 23.6 %copy-start = (bf16[512,1,128]{2,0,1:T(8,128)(2,1)S(1)}, bf16[512,1,128]{2,0,1:T(8,128)(2,1)}, u32[]{:S(2)}) copy-start(bf16[512,1,128]{2,0,1:T(8,128)(2,1)} %param.16) | copy-start | bytes 393220
  12.6 14.4 %copy-start.8 = (s32[10]{0:T(128)S(1)}, s32[10]{0:T(128)}, u32[]{:S(2)}) copy-start(s32[10]{0:T(128)} %constant.70) | copy-start | bytes 124
  12.6 15.0 %copy-start.7 = (s32[10]{0:T(128)S(1)}, s32[10]{0:T(128)}, u32[]{:S(2)}) copy-start(s32[10]{0:T(128)} %constant.71) | copy-start | bytes 124
  12.6 15.7 %copy-start.9 = (pred[10]{0:T(512)(128)(4,1)S(1)}, pred[10]{0:T(512)(128)(4,1)}, u32[]{:S(2)}) copy-start(pred[10]{0:T(512)(128)(4,1)} %constant.44.clone) | copy-start | bytes 34
  12.6 15.7 %copy-start.5 = (s32[10]{0:T(128)S(1)}, s32[10]{0:T(128)}, u32[]{:S(2)}) copy-start(s32[10]{0:T(128)} %constant.20.clone) | copy-start | bytes 124
  12.6 15.7 %copy-start.6 = (s32[10]{0:T(128)S(1)}, s32[10]{0:T(128)}, u32[]{:S(2)}) copy-start(s32[10]{0:T(128)} %constant.19.clone) | copy-start | bytes 124
  12.6 16.3 %copy-start.1 = (bf16[512,1,1024]{2,0,1:T(8,128)(2,1)S(1)}, bf16[512,1,1024]{2,0,1:T(8,128)(2,1)}, u32[]{:S(2)}) copy-start(bf16[512,1,1024]{2,0,1:T(8,128)(2,1)} %param.15) | copy-start | bytes 3145732
  12.6 16.9 %copy-start.2 = (bf16[512,1,1024]{2,0,1:T(8,128)(2,1)S(1)}, bf16[512,1,1024]{2,0,1:T(8,128)(2,1)}, u32[]{:S(2)}) copy-start(bf16[512,1,1024]{2,0,1:T(8,128)(2,1)} %param.18) | copy-start | bytes 3145732
  12.6 17.4 %copy-start.3 = (bf16[1,8,512]{2,1,0:T(8,128)(2,1)S(1)}, bf16[1,8,512]{2,1,0:T(8,128)(2,1)}, u32[]{:S(2)}) copy-start(bf16[1,8,512]{2,1,0:T(8,128)(2,1)} %param.19) | copy-start | bytes 24580
  12.6 17.5 %copy-start.4 = (bf16[1,8,512]{2,1,0:T(8,128)(2,1)S(1)}, bf16[1,8,512]{2,1,0:T(8,128)(2,1)}, u32[]{:S(2)}) copy-start(bf16[1,8,512]{2,1,0:T(8,128)(2,1)} %param.20) | copy-start | bytes 24580
  12.6 244.2 %all-to-all-start = ((bf16[64,64,1,1280]{3,1,2,0:T(8,128)(2,1)}), bf16[64,64,1,1280]{3,1,2,0:T(8,128)(2,1)}, u32[]{:S(2)}, u32[]{:S(2)}) async-start(bf16[64,64,1,1280]{3,1,2,0:T(8,128)(2,1)} %stack.2), calls=%async_computation | async-start | bytes 20971520 | tf_op jit(solution)/shard_map/all_to_all | solution.py:67
  26.1 288.2 %reduce-scatter.2.cloned.1.call-start = ((), (), s32[]{:S(2)}) async-start(), calls=%async_computation.2 | async-start | bytes 5242880 | tf_op jit(solution)/shard_map/reduce_scatter | solution.py:115
  30.1 1.3 copy-start.10
  37.1 219.8 %copy-start.11 = (bf16[512,128]{0,1:T(8,128)(2,1)S(1)}, bf16[512,128]{0,1:T(8,128)(2,1)}, u32[]{:S(2)}) copy-start(bf16[512,128]{0,1:T(8,128)(2,1)} %fusion.22) | copy-start | bytes 393220
Sparse Core Ops, SparseCore 0:
  268.2 46.1 reduce-scatter.1
